TPU v7x, 32 devices: a whole 2x2x4 slice. The times are simulated.
32 devices in a mesh: win: 2 (over y), tm: 4 (over z), row: 2 (over x), col: 2 (over core).
Axes of the slice: x: 2, y: 2, z: 4, core: 2. Of those that a mesh axis runs over, the one named last changes fastest.
Arguments:
- seams: bfloat16 [8, 3, 576, 1920], P(('win', 'tm'), None, 'row', 'col'), parts along dimension 0, may hold values from -24 to 24
- levels: int32 [8, 8, 16], P(('win', 'tm'), 'row', 'col'), parts along dimension 0, may hold values from 0 to 4
- weights: int32 [8], P('win'), parts along dimension 0, may hold values from 16 to 2047
Outputs:
- correction: float32 [8, 3, 576, 1920], P(('win', 'tm'), None, 'row', 'col'), parts along dimension 0
There are 2 independent parts, one for each index of `win`. A program takes and returns all parts, laid end to end along the dimension named above; each array names one. Nothing has to cross between parts.
All inputs are finite; a program needn't handle non-finite values.
Results may differ from a plain program's by a relative error of at most 0.0064.
Values may be sent and summed in bfloat16 or wider, within the bound.
A program may use at most 64 MiB of HBM per device.

v0:
```python
import math

import jax
import jax.numpy as jnp
from jax import lax
from jax.sharding import PartitionSpec as P

screen = 0.001


def cosine_table(length_all, mode_count, cell_first, cell_count):
    mode_ids = jnp.arange(mode_count, dtype=jnp.int32)
    cell_ids = cell_first + jnp.arange(cell_count, dtype=jnp.int32)
    phases = (2 * cell_ids[None, :] + 1) * mode_ids[:, None] % (4 * length_all)
    angles = phases.astype(jnp.float32) * (math.pi / (2.0 * length_all))
    scales = jnp.where(
        mode_ids == 0, math.sqrt(1.0 / length_all), math.sqrt(2.0 / length_all)
    ).astype(jnp.float32)
    return (jnp.cos(angles) * scales[:, None]).astype(jnp.bfloat16)


def laplace_eigen(length_all, mode_first, mode_count):
    mode_ids = (mode_first + jnp.arange(mode_count, dtype=jnp.int32)).astype(jnp.float32)
    sines = jnp.sin(mode_ids * (math.pi / (2.0 * length_all)))
    return 4.0 * sines * sines


def couplings(weights):
    stiff = weights.astype(jnp.float32) / 256.0
    couple = 2.0 * stiff[:-1] * stiff[1:] / (stiff[:-1] + stiff[1:])
    zeroes = jnp.zeros((1,), jnp.float32)
    return (jnp.concatenate([zeroes, couple]), jnp.concatenate([couple, zeroes]))


def local(seams, levels, weights):
    frames_here, channels, rows_here, cols_here = seams.shape
    row_count = lax.axis_size("row")
    col_count = lax.axis_size("col")
    tm_count = lax.axis_size("tm")
    full_height = rows_here * row_count
    full_width = cols_here * col_count
    tile_rows = rows_here // levels.shape[1]
    tile_cols = cols_here // levels.shape[2]
    tile_grid = levels.astype(jnp.float32) * 0.25
    tile_grid = jnp.broadcast_to(
        tile_grid[:, :, None, :, None],
        (frames_here, levels.shape[1], tile_rows, levels.shape[2], tile_cols),
    ).reshape(frames_here, rows_here, cols_here)
    blended = (seams.astype(jnp.float32) * tile_grid[:, None]).astype(jnp.bfloat16)
    flattened = blended.reshape(frames_here * channels * rows_here, cols_here)
    col_first = lax.axis_index("col") * cols_here
    modes_col = full_width // col_count
    mode_first = lax.axis_index("col") * modes_col
    contract_last = (((1,), (1,)), ((), ()))
    cosines = cosine_table(full_width, modes_col * lax.axis_size("col"), col_first, cols_here)
    spectrum_w = lax.psum_scatter(
        lax.dot_general(cosines, flattened, contract_last, preferred_element_type=jnp.float32),
        "col",
        scatter_dimension=0,
        tiled=True,
    )
    spectrum_w = spectrum_w.astype(jnp.bfloat16)
    by_rows = lax.all_to_all(spectrum_w, "row", split_axis=0, concat_axis=1, tiled=True)
    modes_here = modes_col // row_count
    table_h = cosine_table(full_height, full_height, 0, full_height).reshape(
        full_height, row_count, rows_here
    )
    stacked = by_rows.reshape(modes_here, row_count, frames_here, channels, rows_here)
    spectrum = jnp.einsum(
        "qra,wrfca->fqwc", table_h, stacked, preferred_element_type=jnp.float32
    ).reshape(frames_here, full_height, modes_here * channels)
    eigen_cols = laplace_eigen(
        full_width, mode_first + lax.axis_index("row") * modes_here, modes_here
    )
    couple_below, couple_above = couplings(weights)
    tm_index = lax.axis_index("tm")
    per_tm = full_height // tm_count
    by_frames = lax.all_to_all(spectrum, "tm", split_axis=1, concat_axis=0, tiled=True)
    eigen_rows = laplace_eigen(full_height, tm_index * per_tm, per_tm)
    narrow = eigen_rows[:, None] + eigen_cols[None, :]
    eigen_sum = jnp.broadcast_to(narrow[..., None], narrow.shape + (channels,)).reshape(
        narrow.shape[:-1] + (modes_here * channels,)
    )

    def descend(carried, inputs):
        ratio_prev, value_prev = carried
        source, below_now, above_now = inputs
        pivot = screen + eigen_sum + below_now + above_now - below_now * ratio_prev
        value_now = (source + below_now * value_prev) / pivot
        ratio_now = above_now / pivot
        return ((ratio_now, value_now), (ratio_now, value_now))

    zeroes = jnp.zeros_like(eigen_sum)
    _, (ratios, reduced) = lax.scan(
        descend, (zeroes, zeroes), (by_frames, couple_below, couple_above)
    )

    def ascend(following, inputs):
        ratio_now, value_now = inputs
        result = value_now + ratio_now * following
        return (result, result)

    _, solved_frames = lax.scan(ascend, zeroes, (ratios, reduced), reverse=True)
    solved = lax.all_to_all(
        solved_frames.astype(jnp.bfloat16), "tm", split_axis=0, concat_axis=1, tiled=True
    ).astype(solved_frames.dtype)
    solved_low = solved.astype(jnp.bfloat16).reshape(frames_here, full_height, modes_here, channels)
    restored = jnp.einsum(
        "qra,fqwc->wrfca", table_h, solved_low, preferred_element_type=jnp.float32
    ).astype(jnp.bfloat16)
    restored = restored.reshape(modes_here, row_count * frames_here * channels * rows_here)
    restored = lax.all_to_all(restored, "row", split_axis=1, concat_axis=0, tiled=True)
    segment = lax.all_gather(restored, "col", axis=0, tiled=True)
    cosines = cosine_table(full_width, segment.shape[0], col_first, cols_here)
    result = lax.dot_general(
        segment, cosines, (((0,), (0,)), ((), ())), preferred_element_type=jnp.float32
    )
    return result.reshape(frames_here, channels, rows_here, cols_here)


def solution(mesh):
    placed = (P(("win", "tm"), None, "row", "col"), P(("win", "tm"), "row", "col"), P("win"))
    return jax.shard_map(
        local,
        mesh=mesh,
        in_specs=placed,
        out_specs=P(("win", "tm"), None, "row", "col"),
        check_vma=False,
    )
```

profile of v0, /device:TPU:1, one launch (start us, length us, event | category | flops | bytes accessed | tf_op | source)
XLA Modules:
  0.0 432.7 jit_solution(1388305950070247697)
XLA Ops:
  7.7 2.0 multiply_convert_fusion
  9.7 34.2 %fusion.15 = f32[1920,864]{1,0:T(8,128)} fusion(bf16[864,960]{1,0:T(8,128)(2,1)S(1)} %bitcast.80, f32[1920]{0:T(1024)S(1)} %fusion.51, s32[960]{0:T(1024)S(1)} %multiply_add_fusion), kind=kOutput, calls=%fused_computation.24 | convolution fusion | flops 3205324800 | bytes 8305920 | tf_op jit(solution)/shard_map/dot_general | solution.py:57
  43.9 18.3 %reduce-scatter.2.cloned.1.call-done = f32[960,864]{1,0:T(8,128)} async-done(((f32[1920,864]{1,0:T(8,128)}), f32[960,864]{1,0:T(8,128)}) %reduce-scatter.2.cloned.1.call-update) | async-done | bytes 3317776 | tf_op jit(solution)/shard_map/reduce_scatter | solution.py:56
  62.2 3.3 convert_element_type.99
  65.5 3.9 all-to-all-start
  70.0 20.1 %all-to-all-done = bf16[2,480,864]{2,1,0:T(8,128)(2,1)S(1)} async-done(((bf16[2,480,864]{2,1,0:T(8,128)(2,1)}), bf16[2,480,864]{2,1,0:T(8,128)(2,1)S(1)}, u32[]{:S(2)}, u32[]{:S(2)}) %all-to-all-start) | async-done | bytes 1658912 | tf_op jit(solution)/shard_map/all_to_all | solution.py:63
  90.1 2.3 copy.31
  92.4 8.2 %convolution_bitcast_fusion = f32[1,576,480,3]{2,1,3,0:T(8,128)S(1)} fusion(bf16[480,2,3,288]{0,3,2,1:T(8,128)(2,1)} %bitcast.81, f32[576]{0:T(1024)S(1)} %fusion.52, s32[2,288]{1,0:T(2,128)} %multiply_add_fusion.1), kind=kOutput, calls=%fused_computation.28 | convolution fusion | flops 959164416 | bytes 4981248 | tf_op jit(solution)/shard_map/qra,wrfca->fqwc/dot_general | solution.py:69
  100.6 6.0 %copy.32 = f32[1,576,480,3]{1,0,3,2:T(1,128)} copy(f32[1,576,480,3]{2,1,3,0:T(8,128)S(1)} %convolution_bitcast_fusion) | data formatting | bytes 6635520 | tf_op jit(solution)/shard_map/qra,wrfca->fqwc/transpose | solution.py:69
  106.6 12.8 %copy.33 = f32[1,576,1440]{2,0,1:T(1,128)} copy(f32[1,576,1440]{1,0,2:T(1,128)} %bitcast.76) | data formatting | bytes 6635520 | tf_op jit(solution)/shard_map/reshape | solution.py:71
  119.4 4.8 %all-to-all-start.1 = ((f32[1,576,1440]{2,0,1:T(1,128)}), f32[1,576,1440]{2,0,1:T(1,128)}, u32[]{:S(2)}, u32[]{:S(2)}) async-start(f32[1,576,1440]{2,0,1:T(1,128)} %copy.33), calls=%async_computation.2 | async-start | bytes 7077888 | tf_op jit(solution)/shard_map/all_to_all | solution.py:78
  127.2 75.8 %all-to-all-done.1 = f32[1,576,1440]{2,0,1:T(1,128)} async-done(((f32[1,576,1440]{2,0,1:T(1,128)}), f32[1,576,1440]{2,0,1:T(1,128)}, u32[]{:S(2)}, u32[]{:S(2)}) %all-to-all-start.1) | async-done | bytes 3317792 | tf_op jit(solution)/shard_map/all_to_all | solution.py:78
  202.9 4.0 copy.54
  206.9 2.2 broadcast.234
  209.1 2.2 broadcast.234.clone.1
  211.4 66.3 %while.34 = (s32[]{:T(128)}, f32[144,1440]{0,1:T(8,128)S(1)}, f32[144,1440]{0,1:T(8,128)}, f32[4,144,1440]{2,1,0:T(8,128)}, f32[4,144,1440]{2,1,0:T(8,128)}, /*i...) while((s32[]{:T(128)}, f32[144,1440]{0,1:T(8,128)S(1)}, ...), condition=%wide.region_2.3_spmd.clone, body=%wide.region_1.2_spmd.clone.sunk | while | flops 2280963 | bytes 17805980 | solution.py:94
  218.5 5.6 %fusion.73 = (f32[144,1440]{0,1:T(8,128)}, f32[144,1440]{0,1:T(8,128)S(1)}) fusion(f32[1,144,1440]{1,2,0:T(8,128)} %copy.62, f32[144,1440]{0,1:T(8,128)} %get-tuple-element.399, f32[]{:T(128)} %bitcast.68, pred[]{:T(512)S(6)} %compare.6, f32[144,1440]{0,1:T(8,128)S(1)} %get-tuple-element.398, f32[]{:T(128)} %bitcast.69, f32[144,1440]{0,1:T(8,128)} %reshape.196), kind=kLoop, calls=%fused_computation.2.clone.1 | loop fusion | flops 2280960 | bytes 4976649 | tf_op jit(solution)/shard_map/while/body/eval_jaxpr/div | solution.py:89
  234.7 6.0 %fusion.73 = (f32[144,1440]{0,1:T(8,128)}, f32[144,1440]{0,1:T(8,128)S(1)}) fusion(f32[1,144,1440]{1,2,0:T(8,128)} %copy.62, f32[144,1440]{0,1:T(8,128)} %get-tuple-element.399, f32[]{:T(128)} %bitcast.68, pred[]{:T(512)S(6)} %compare.6, f32[144,1440]{0,1:T(8,128)S(1)} %get-tuple-element.398, f32[]{:T(128)} %bitcast.69, f32[144,1440]{0,1:T(8,128)} %reshape.196), kind=kLoop, calls=%fused_computation.2.clone.1 | loop fusion | flops 2280960 | bytes 4976649 | tf_op jit(solution)/shard_map/while/body/eval_jaxpr/div | solution.py:89
  251.4 6.0 %fusion.73 = (f32[144,1440]{0,1:T(8,128)}, f32[144,1440]{0,1:T(8,128)S(1)}) fusion(f32[1,144,1440]{1,2,0:T(8,128)} %copy.62, f32[144,1440]{0,1:T(8,128)} %get-tuple-element.399, f32[]{:T(128)} %bitcast.68, pred[]{:T(512)S(6)} %compare.6, f32[144,1440]{0,1:T(8,128)S(1)} %get-tuple-element.398, f32[]{:T(128)} %bitcast.69, f32[144,1440]{0,1:T(8,128)} %reshape.196), kind=kLoop, calls=%fused_computation.2.clone.1 | loop fusion | flops 2280960 | bytes 4976649 | tf_op jit(solution)/shard_map/while/body/eval_jaxpr/div | solution.py:89
  268.1 6.0 %fusion.73 = (f32[144,1440]{0,1:T(8,128)}, f32[144,1440]{0,1:T(8,128)S(1)}) fusion(f32[1,144,1440]{1,2,0:T(8,128)} %copy.62, f32[144,1440]{0,1:T(8,128)} %get-tuple-element.399, f32[]{:T(128)} %bitcast.68, pred[]{:T(512)S(6)} %compare.6, f32[144,1440]{0,1:T(8,128)S(1)} %get-tuple-element.398, f32[]{:T(128)} %bitcast.69, f32[144,1440]{0,1:T(8,128)} %reshape.196), kind=kLoop, calls=%fused_computation.2.clone.1 | loop fusion | flops 2280960 | bytes 4976649 | tf_op jit(solution)/shard_map/while/body/eval_jaxpr/div | solution.py:89
  277.6 11.7 %while.35 = (s32[]{:T(128)}, f32[144,1440]{1,0:T(8,128)}, bf16[4,144,1440]{2,1,0:T(8,128)(2,1)}, f32[4,144,1440]{2,1,0:T(8,128)}, f32[4,144,1440]{2,1,0:T(8,128)}, /*index=5*/s32[]{:T(128)}, s32[]{:T(128)}, s32[]{:T(128)}) while((s32[]{:T(128)}, f32[144,1440]{1,0:T(8,128)}, bf16[4,144,1440]{2,1,0:T(8,128)(2,1)}, ...), condition=%wide.region_4.5_spmd.clone, body=%wide.region_3.4_spmd.clone.sunk | while | flops 622084 | bytes 4423791 | solution.py:103
  277.6 2.7 bitcast_dynamic-update-slice_fusion.2
  280.4 3.0 bitcast_dynamic-update-slice_fusion.2
  283.4 3.0 bitcast_dynamic-update-slice_fusion.2
  286.4 3.0 bitcast_dynamic-update-slice_fusion.2
  289.3 44.9 %all_to_all.56 = bf16[4,144,1440]{2,1,0:T(8,128)(2,1)} all-to-all(bf16[4,144,1440]{2,1,0:T(8,128)(2,1)} %get-tuple-element.158), channel_id=1, replica_groups=mesh['win'=2,'tm'=4,'row'=2,'col'=2] {'tm'}, dimensions={0} | all-to-all | bytes 3317760 | tf_op jit(solution)/shard_map/all_to_all | solution.py:104
  334.2 4.6 %copy.39 = bf16[4,144,1440]{1,0,2:T(4,128)(2,1)S(1)} copy(bf16[4,144,1440]{2,1,0:T(8,128)(2,1)} %all_to_all.56) | data formatting | bytes 3317760 | tf_op jit(solution)/shard_map/all_to_all | solution.py:104
  338.8 4.8 %reshape.185 = bf16[576,480,3]{0,2,1:T(4,128)(2,1)} reshape(bf16[4,144,1440]{1,0,2:T(4,128)(2,1)S(1)} %copy.39) | data formatting | bytes 3317760 | tf_op jit(solution)/shard_map/reshape.18
  343.6 8.9 %convert_bitcast_fusion = bf16[480,2,1,3,288]{0,4,1,3,2:T(8,128)(2,1)S(1)} fusion(bf16[576,480,3,1]{0,2,1,3:T(4,128)(2,1)} %bitcast.79, f32[576]{0:T(1024)S(1)} %fusion.52, s32[2,288]{1,0:T(2,128)S(1)} %copy-done), kind=kOutput, calls=%fused_computation.31 | convolution fusion | flops 959993856 | bytes 3322368 | tf_op jit(solution)/shard_map/qra,fqwc->wrfca/dot_general | solution.py:108
  354.1 22.6 %all_to_all.57 = bf16[480,2,864]{2,0,1:T(8,128)(2,1)} all-to-all(bf16[480,2,864]{2,0,1:T(8,128)(2,1)S(1)} %copy.42), channel_id=1, replica_groups=mesh['win'=2,'tm'=4,'row'=2,'col'=2] {'row'}, dimensions={1} | all-to-all | bytes 3317760 | tf_op jit(solution)/shard_map/all_to_all | solution.py:112
  376.7 13.4 %all-gather.2.cloned.1.call-done = bf16[1920,864]{1,0:T(8,128)(2,1)} async-done(((bf16[960,864]{1,0:T(8,128)(2,1)}), bf16[1920,864]{1,0:T(8,128)(2,1)}) %all-gather.2.cloned.1.call-update) | async-done | bytes 3317776 | tf_op jit(solution)/shard_map/all_gather | solution.py:113
  390.1 35.3 %fusion.13 = f32[864,960]{1,0:T(8,128)} fusion(bf16[1920,864]{1,0:T(8,128)(2,1)} %all-gather.2.cloned.1.call-done, f32[1920]{0:T(1024)S(1)} %fusion.51, s32[960]{0:T(1024)S(1)} %multiply_add_fusion), kind=kOutput, calls=%fused_computation.23 | convolution fusion | flops 3205324800 | bytes 6647040 | tf_op jit(solution)/shard_map/dot_general | solution.py:115
  (63 shorter events, 48.9 us)
Async XLA Ops:
  6.5 55.6 %reduce-scatter.2.cloned.1.call-start = ((), (), s32[]{:S(2)}) async-start(), calls=%async_computation.5 | async-start | bytes 10321920 | tf_op jit(solution)/shard_map/reduce_scatter | solution.py:56
  65.5 24.5 %all-to-all-start = ((bf16[2,480,864]{2,1,0:T(8,128)(2,1)}), bf16[2,480,864]{2,1,0:T(8,128)(2,1)S(1)}, u32[]{:S(2)}, u32[]{:S(2)}) async-start(bf16[2,480,864]{2,1,0:T(8,128)(2,1)} %bitcast.2), calls=%async_computation.1 | async-start | bytes 3440640 | tf_op jit(solution)/shard_map/all_to_all | solution.py:63
  119.4 5.2 %copy-start.1 = (s32[4]{0:T(128)S(1)}, s32[4]{0:T(128)}, u32[]{:S(2)}) copy-start(s32[4]{0:T(128)} %param.9) | copy-start | bytes 52
  119.4 83.6 %all-to-all-start.1 = ((f32[1,576,1440]{2,0,1:T(1,128)}), f32[1,576,1440]{2,0,1:T(1,128)}, u32[]{:S(2)}, u32[]{:S(2)}) async-start(f32[1,576,1440]{2,0,1:T(1,128)} %copy.33), calls=%async_computation.2 | async-start | bytes 7077888 | tf_op jit(solution)/shard_map/all_to_all | solution.py:78
  124.2 265.9 %all-gather.2.cloned.1.call-start = ((), (), s32[]{:S(2)}) async-start(), calls=%async_computation.6 | async-start | bytes 5160960 | tf_op jit(solution)/shard_map/all_gather | solution.py:113
  338.8 4.8 %copy-start = (s32[2,288]{1,0:T(2,128)S(1)}, s32[2,288]{1,0:T(2,128)}, u32[]{:S(2)}) copy-start(s32[2,288]{1,0:T(2,128)} %multiply_add_fusion.1) | copy-start | bytes 6916
Sparse Core Ops, SparseCore 0:
  44.0 18.0 reduce-scatter.1
  376.9 13.2 all-gather.1
where the time goes:
time: 441 us; the launch traced here: 433 us
  waiting for transfers between devices  128 us (29%)
  matrix products  86.6 us (20%)
  local copies, waits for them, and re-layouts  83.6 us (19%)
  blocking collectives  67.5 us (15%)
  other arithmetic  44.5 us (10%)
  between operations  14 us (3%)
  starting transfers between devices  8.96 us (2%)
    all_to_all x1, waiting for transfers between devices, local(): lax.all_to_all(spectrum, 'tm', split_axis=1, concat_axis=0, tiled=True)  75.8 us
    all_to_all x1, blocking collectives, local(): lax.all_to_all(solved_frames.astype(jnp.bfloat16), 'tm', split_axis=0, co...  44.9 us
    dot_general x1, matrix products, local(): lax.dot_general(segment, cosines, (((0,), (0,)), ((), ())), preferred_ele...  35.3 us
    dot_general x1, matrix products, local(): lax.dot_general(cosines, flattened, contract_last, preferred_element_type...  34.2 us
    div x4, other arithmetic, descend(): value_now = (source + below_now * value_prev) / pivot  23.6 us
    all_to_all x1, blocking collectives, local(): lax.all_to_all(restored, 'row', split_axis=1, concat_axis=0, tiled=True)  22.6 us
    all_to_all x1, waiting for transfers between devices, local(): lax.all_to_all(spectrum_w, 'row', split_axis=0, concat_axis=1, tiled=True)  20.1 us
    reduce_scatter x1, waiting for transfers between devices, local(): lax.psum_scatter(lax.dot_general(cosines, flattened, contract_last, prefe...  18.3 us
  transfers between devices with their start and end apart: 4, of which 4 were waited for; matrix products, arithmetic and copies ran while one was open for 1% of the time, Pallas kernels for 0%

commit v1 on v0

v1 whole, which is shorter than its diff:
```python
import functools
import math

import jax
import jax.numpy as jnp
from jax import lax
from jax.experimental import pallas as pl
from jax.experimental.pallas import tpu as pltpu
from jax.sharding import PartitionSpec as P

screen = 0.001
LANES = 128
MESH = pl.DeviceIdType.MESH


def scales_of(length_all, mode_ids, valid=None):
    scales = jnp.where(
        mode_ids == 0, math.sqrt(1.0 / length_all), math.sqrt(2.0 / length_all)
    ).astype(jnp.float32)
    return scales if valid is None else jnp.where(valid, scales, 0.0)


def angles_of(length_all, products):
    return (products % (4 * length_all)).astype(jnp.float32) * (math.pi / (2.0 * length_all))


def table_cells_by_modes(length_all, cell_first, cell_count, mode_ids, scales):
    step = 24
    mode_ids = mode_ids[..., None, :]
    coarse = 2 * step * jnp.arange(cell_count // step, dtype=jnp.int32)[:, None]
    fine = 2 * (cell_first + jnp.arange(step, dtype=jnp.int32))[:, None] + 1
    angle_a = angles_of(length_all, coarse * mode_ids)
    angle_b = angles_of(length_all, fine * mode_ids)
    scales = scales[..., None, :]
    cos_a, sin_a = jnp.cos(angle_a), jnp.sin(angle_a)
    cos_b, sin_b = jnp.cos(angle_b) * scales, jnp.sin(angle_b) * scales
    table = (
        cos_a[..., :, None, :] * cos_b[..., None, :, :]
        - sin_a[..., :, None, :] * sin_b[..., None, :, :]
    )
    return table.reshape(table.shape[:-3] + (cell_count, table.shape[-1])).astype(jnp.bfloat16)


def table_modes_by_cells(length_all, bases, step, scales, cell_first, cell_count):
    odd = 2 * (cell_first + jnp.arange(cell_count, dtype=jnp.int32))[None, :] + 1
    angle_a = angles_of(length_all, bases[:, None] * odd)
    angle_b = angles_of(length_all, jnp.arange(step, dtype=jnp.int32)[:, None] * odd)
    cos_a, sin_a = jnp.cos(angle_a), jnp.sin(angle_a)
    cos_b, sin_b = jnp.cos(angle_b), jnp.sin(angle_b)
    table = cos_a[:, None] * cos_b[None] - sin_a[:, None] * sin_b[None]
    table = table * scales[:, :, None]
    return table.reshape(-1, cell_count).astype(jnp.bfloat16)


def laplace_eigen(length_all, mode_ids):
    sines = jnp.sin(mode_ids.astype(jnp.float32) * (math.pi / (2.0 * length_all)))
    return 4.0 * sines * sines


def kernel(J, R, n, C, M, x_ref, twf, twb, thf, tht, dd, ee, cpl, o_ref,
           xg, sw, sr, u, yb, yin, zin, xb, rb, rg, out,
           g_s, g_r, f_s, f_r, y_s, y_r, z_r, x_s, b_s, b_r, c_s, c_r, o_s):
    j, r, t = lax.axis_index("col"), lax.axis_index("row"), lax.axis_index("tm")
    N = C * M
    left = t < n // 2
    p = jnp.where(left, t, n - 1 - t)
    inner = jnp.where(left, t + 1, t - 1)
    outer = jnp.where(left, t - 1, t + 1)
    edge = p == 0
    mid = p == n // 2 - 1

    barrier = pltpu.get_barrier_semaphore()
    for d in range(1, J):
        pl.semaphore_signal(barrier, 1, device_id={"col": lax.rem(j + d, J)}, device_id_type=MESH)
    for d in range(1, R):
        pl.semaphore_signal(barrier, 1, device_id={"row": lax.rem(r + d, R)}, device_id_type=MESH)
    pl.semaphore_signal(barrier, 1, device_id={"tm": inner}, device_id_type=MESH)

    @pl.when(p > 0)
    def _():
        pl.semaphore_signal(barrier, 1, device_id={"tm": outer}, device_id_type=MESH)
        pl.semaphore_wait(barrier, J + R)

    @pl.when(p == 0)
    def _():
        pl.semaphore_wait(barrier, J + R - 1)

    def remote(src, dst, ss, rs, where):
        return pltpu.make_async_remote_copy(
            src_ref=src, dst_ref=dst, send_sem=ss, recv_sem=rs,
            device_id=where, device_id_type=MESH)

    def slot(jj, rr, m):
        return pl.ds(pl.multiple_of(((jj * R + rr) * M + m) * LANES, LANES), LANES)

    def gather(c, d):
        return remote(x_ref.at[c], xg.at[c, d - 1], g_s.at[c, d - 1], g_r.at[c, d - 1],
                      {"col": lax.rem(j + d, J)})

    def row_out(i, d):
        peer = lax.rem(r + d, R)
        return remote(sw.at[i, peer], sr.at[i, d - 1], f_s.at[i, d - 1], f_r.at[i, d - 1],
                      {"row": peer})

    def y_inner(i):
        return remote(yb.at[i], yin.at[i], y_s.at[i], y_r.at[i], {"tm": inner})

    def y_middle(i):
        return remote(yb.at[i], zin.at[i], y_s.at[i], z_r.at[i], {"tm": inner})

    def x_outer(i):
        return remote(xb.at[i], zin.at[i], x_s.at[i], z_r.at[i], {"tm": outer})

    def row_back(i, c, m, d):
        return remote(rb.at[i, d - 1], rg.at[c, :, slot(j, r, m)], b_s.at[i, d - 1],
                      b_r.at[i, d - 1], {"row": lax.rem(r + d, R)})

    def col_share(i, c, m, d, e):
        part = rg.at[c, :, slot(j, lax.rem(r + R - d, R), m)]
        return remote(part, part, c_s.at[i, d, e - 1], c_r.at[i, d, e - 1],
                      {"col": lax.rem(j + e, J)})

    def out_copy(c):
        return pltpu.make_async_copy(out.at[c], o_ref.at[c], o_s.at[c])

    for c in range(C):
        for d in range(1, J):
            gather(c, d).start()

    def dot(a, b):
        return jnp.dot(a, b, preferred_element_type=jnp.float32)

    def step(i, carry):
        @pl.when(i < N)
        def _():
            c, m = i // M, i % M

            @pl.when(m == 0)
            def _():
                for d in range(1, J):
                    gather(c, d).wait_recv()
            acc = dot(x_ref[c], twf[0, m])
            for d in range(1, J):
                acc += dot(xg[c, d - 1], twf[d, m])
            low = acc.astype(jnp.bfloat16)
            for rr in range(R):
                sw[i, rr] = low[:, rr * LANES:(rr + 1) * LANES]
            for d in range(1, R):
                row_out(i, d).start()

        ib = i - 1

        @pl.when((ib >= 0) & (ib < N))
        def _():
            acc = dot(thf[r], sw[ib, r])
            for d in range(1, R):
                row_out(ib, d).wait_recv()
                acc += dot(thf[lax.rem(r + R - d, R)], sr[ib, d - 1])
            u[ib] = acc

        ic = i - 1 - p

        @pl.when((ic >= 0) & (ic < N))
        def _():
            @pl.when(p > 0)
            def _():
                y_inner(ic).wait_recv()
                u[ic] = u[ic] + cpl[0] * yin[ic].astype(jnp.float32)
            yb[ic] = (u[ic] * dd[ic % M]).astype(jnp.bfloat16)

            @pl.when(mid)
            def _():
                y_middle(ic).start()

            @pl.when(jnp.logical_not(mid))
            def _():
                y_inner(ic).start()

        ix = i - n + p

        @pl.when((ix >= 0) & (ix < N))
        def _():
            c, m = ix // M, ix % M
            x_outer(ix).wait_recv()
            x = ((u[ix] + cpl[1] * zin[ix].astype(jnp.float32)) * ee[m]).astype(jnp.bfloat16)
            xb[ix] = x

            @pl.when(p > 0)
            def _():
                x_outer(ix).start()
            for d in range(1, R):
                rb[ix, d - 1] = dot(tht[lax.rem(r + d, R)], x).astype(jnp.bfloat16)
                row_back(ix, c, m, d).start()
            rg[c, :, slot(j, r, m)] = dot(tht[r], x).astype(jnp.bfloat16)
            for e in range(1, J):
                col_share(ix, c, m, 0, e).start()

        iw = ix - 1

        @pl.when((iw >= 0) & (iw < N))
        def _():
            c, m = iw // M, iw % M
            for d in range(1, R):
                row_back(iw, c, m, d).wait_recv()
                for e in range(1, J):
                    col_share(iw, c, m, d, e).start()

        ig = ix - 2

        @pl.when((ig >= 0) & (ig < N))
        def _():
            c, m = ig // M, ig % M
            for d in range(R):
                for e in range(1, J):
                    col_share(ig, c, m, d, e).wait_recv()

            @pl.when(m == M - 1)
            def _():
                out[c] = dot(rg[c], twb[...])
                out_copy(c).start()
        return carry

    lax.fori_loop(0, N + n + 2, step, 0)

    def drain(i, carry):
        c, m = i // M, i % M
        for d in range(1, R):
            row_out(i, d).wait_send()
            row_back(i, c, m, d).wait_send()
        for d in range(R):
            for e in range(1, J):
                col_share(i, c, m, d, e).wait_send()
        y_inner(i).wait_send()

        @pl.when(p > 0)
        def _():
            x_outer(i).wait_send()
        return carry

    lax.fori_loop(0, N, drain, 0)
    for c in range(C):
        for d in range(1, J):
            gather(c, d).wait_send()
        out_copy(c).wait()


def local(seams, levels, weights):
    _, C, rows, cols = seams.shape
    R, J, n = lax.axis_size("row"), lax.axis_size("col"), lax.axis_size("tm")
    j, r, t = lax.axis_index("col"), lax.axis_index("row"), lax.axis_index("tm")
    H, W = rows * R, cols * J
    tile_rows, tile_cols = rows // levels.shape[1], cols // levels.shape[2]
    grid = levels[0].astype(jnp.float32) * 0.25
    grid = jnp.broadcast_to(
        grid[:, None, :, None], (levels.shape[1], tile_rows, levels.shape[2], tile_cols)
    ).reshape(rows, cols)
    blended = (seams[0].astype(jnp.float32) * grid[None]).astype(jnp.bfloat16)

    modes = W // (J * R)
    M = -(-modes // LANES)
    N = C * M
    lanes = jnp.arange(M * LANES, dtype=jnp.int32).reshape(M, LANES)
    valid = lanes < modes
    blocks = jnp.arange(R, dtype=jnp.int32)[None, :, None] * modes
    mode_f = (j * R * modes + blocks + lanes[:, None, :]).reshape(M, R * LANES)
    valid_f = jnp.broadcast_to(valid[:, None, :], (M, R, LANES)).reshape(M, R * LANES)
    scale_f = scales_of(W, mode_f, valid_f)
    twf = jnp.stack([
        table_cells_by_modes(W, lax.rem(j + J - d, J) * cols, cols, mode_f, scale_f)
        for d in range(J)])

    fine = 16
    bases = (jnp.arange(J * R, dtype=jnp.int32)[:, None] * modes
             + jnp.arange(M * LANES // fine, dtype=jnp.int32)[None, :] * fine).reshape(-1)
    mode_b = (jnp.arange(J * R, dtype=jnp.int32)[:, None] * modes
              + jnp.arange(M * LANES, dtype=jnp.int32)[None, :])
    valid_b = jnp.broadcast_to(valid.reshape(1, -1), mode_b.shape)
    scale_b = scales_of(W, mode_b, valid_b).reshape(-1, fine)
    twb = table_modes_by_cells(W, bases, fine, scale_b, j * cols, cols)

    mode_h = jnp.arange(H, dtype=jnp.int32)
    tht = table_cells_by_modes(H, 0, H, mode_h, scales_of(H, mode_h))
    thf = tht.T.reshape(H, R, rows).transpose(1, 0, 2)
    tht = tht.reshape(R, rows, H)

    own_modes = (j * R + r) * modes + lanes
    a = (screen + laplace_eigen(H, mode_h)[None, :, None]
         + laplace_eigen(W, own_modes)[:, None, :])
    stiff = weights.astype(jnp.float32) / 256.0
    couple = 2.0 * stiff[:-1] * stiff[1:] / (stiff[:-1] + stiff[1:])
    half = n // 2
    left = t < half
    place = jnp.where(left, t, n - 1 - t)
    ends = jnp.concatenate([jnp.zeros((1,), jnp.float32), couple])
    flipped = jnp.concatenate([jnp.zeros((1,), jnp.float32), couple[::-1]])
    own = jnp.where(left, ends, flipped)
    other = jnp.where(left, flipped, ends)

    def sweep(chain):
        rest = jnp.zeros_like(a)
        first = None
        for k in range(half):
            base = a + chain[k] * rest
            inverse = 1.0 / (base + chain[k + 1])
            first = inverse if first is None else jnp.where(place == k, inverse, first)
            rest = base * inverse
        return base, rest, first

    base, _, dd = sweep(own)
    _, rest_other, _ = sweep(other)
    ee = jnp.where(place == half - 1, 1.0 / (base + own[half] * rest_other), dd)
    cpl = lax.dynamic_slice(own, (place,), (2,))

    bf, f32 = jnp.bfloat16, jnp.float32
    vm, dma = pltpu.VMEM, pltpu.SemaphoreType.DMA
    spec = pl.BlockSpec(memory_space=pltpu.VMEM)
    result = pl.pallas_call(
        functools.partial(kernel, J, R, n, C, M),
        out_shape=jax.ShapeDtypeStruct((C, rows, cols), f32),
        in_specs=[spec] * 7 + [pl.BlockSpec(memory_space=pltpu.SMEM)],
        out_specs=pl.BlockSpec(memory_space=pl.ANY),
        scratch_shapes=[
            vm((C, J - 1, rows, cols), bf),
            vm((N, R, rows, LANES), bf),
            vm((N, R - 1, rows, LANES), bf),
            vm((N, H, LANES), f32),
            vm((N, H, LANES), bf),
            vm((N, H, LANES), bf),
            vm((N, H, LANES), bf),
            vm((N, H, LANES), bf),
            vm((N, R - 1, rows, LANES), bf),
            vm((C, rows, J * R * M * LANES), bf),
            vm((C, rows, cols), f32),
            dma((C, J - 1)), dma((C, J - 1)),
            dma((N, R - 1)), dma((N, R - 1)),
            dma((N,)), dma((N,)), dma((N,)), dma((N,)),
            dma((N, R - 1)), dma((N, R - 1)),
            dma((N, R, J - 1)), dma((N, R, J - 1)),
            dma((C,)),
        ],
        compiler_params=pltpu.CompilerParams(
            collective_id=0, has_side_effects=True, vmem_limit_bytes=60 * 1024 * 1024),
    )(blended, twf, twb, thf, tht, dd, ee, cpl)
    return result[None]


def solution(mesh):
    placed = (P(("win", "tm"), None, "row", "col"), P(("win", "tm"), "row", "col"), P("win"))
    return jax.shard_map(
        local,
        mesh=mesh,
        in_specs=placed,
        out_specs=P(("win", "tm"), None, "row", "col"),
        check_vma=False,
    )
```

time: 441 us -> 122 us (0.28); the launches traced: 433 us -> 122 us
  waiting for transfers between devices: 128 us -> 0 us
  matrix products: 86.6 us -> 0 us
  Pallas kernels: 0 us -> 84.3 us
  local copies, waits for them, and re-layouts: 83.6 us -> 8.25 us
  blocking collectives: 67.5 us -> 0 us
  other arithmetic: 44.5 us -> 27.7 us
  between operations: 14 us -> 1.36 us
  starting transfers between devices: 8.96 us -> 0 us
    all_to_all x2 -> x0, waiting for transfers between devices: 95.8 us -> none  [the longest x1 75.8 us: local(): lax.all_to_all(spectrum, 'tm', split_axis=1, concat_axis=0, tiled=True)]
    dot_general x4 -> x0, matrix products: 86.6 us -> none  [the longest x1 35.3 us: local(): lax.dot_general(segment, cosines, (((0,), (0,)), ((), ())), preferred_ele...]
    pallas_call x0 -> x1, Pallas kernels: none -> 84.3 us  [local(): pl.pallas_call(functools.partial(kernel, J, R, n, C, M), out_shape=jax.Sh...]
    all_to_all x2 -> x0, blocking collectives: 67.5 us -> none  [the longest x1 44.9 us: local(): lax.all_to_all(solved_frames.astype(jnp.bfloat16), 'tm', split_axis=0, co...]
    div x6 -> x2, other arithmetic: 23.7 us -> 0.08 us  [the longest x1 0.08 us: local(): couple = 2.0 * stiff[:-1] * stiff[1:] / (stiff[:-1] + stiff[1:])]
    reshape x5 -> x1, local copies, waits for them, and re-layouts: 19.6 us -> 1.27 us  [local(): thf = tht.T.reshape(H, R, rows).transpose(1, 0, 2)]
    reduce_scatter x1 -> x0, waiting for transfers between devices: 18.3 us -> none  [local(): lax.psum_scatter(lax.dot_general(cosines, flattened, contract_last, prefe...]
    dynamic_slice x16 -> x1, local copies, waits for them, and re-layouts: 16 us -> 0.66 us  [local(): cpl = lax.dynamic_slice(own, (place,), (2,))]
  transfers between devices with their start and end apart: 4 -> 0, of which waited for: 4 -> 0; matrix products, arithmetic and copies ran while one was open for 1% -> 0% of each run, Pallas kernels for 0% -> 0%
where the time goes in v1:
time: 122 us
  Pallas kernels  84.3 us (69%)
  other arithmetic  27.7 us (23%)
  local copies, waits for them, and re-layouts  8.25 us (7%)
  between operations  1.36 us (1%)
    pallas_call x1, Pallas kernels, local(): pl.pallas_call(functools.partial(kernel, J, R, n, C, M), out_shape=jax.Sh...  84.3 us
    convert_element_type x1, other arithmetic, table_modes_by_cells(): return table.reshape(-1, cell_count).astype(jnp.bfloat16)  5.86 us
    select_n x1, other arithmetic, local(): ee = jnp.where(place == half - 1, 1.0 / (base + own[half] * rest_other), dd)  4.92 us
    sub x1, other arithmetic, table_modes_by_cells(): table = cos_a[:, None] * cos_b[None] - sin_a[:, None] * sin_b[None]  4.39 us
    unnamed x6, local copies, waits for them, and re-layouts  4.29 us
    convert_element_type x1, other arithmetic, local(): blended = (seams[0].astype(jnp.float32) * grid[None]).astype(jnp.bfloat16)  3.2 us

profile of v1, /device:TPU:1, one launch (start us, length us, event | category | flops | bytes accessed | tf_op | source)
XLA Modules:
  0.0 121.7 jit_solution(13204845340867093968)
XLA Ops:
  0.0 0.7 multiply_bitcast_fusion
  0.7 0.1 broadcast_in_dim.37
  0.8 0.3 mul.712
  1.2 3.2 %fusion.1.x_ref = bf16[3,288,960]{2,1,0:T(8,128)(2,1)} fusion(bf16[1,3,288,960]{3,2,1,0:T(8,128)(2,1)} %param.3, f32[288,960]{1,0:T(8,128)S(1)} %mul.712), kind=kLoop, calls=%fused_computation.7 | loop fusion | flops 2488320 | bytes 4423680 | tf_op jit(solution)/shard_map/convert_element_type | solution.py:257
  4.4 0.1 broadcast_bitcast_fusion.1
  4.5 0.9 cosine_multiply_fusion.1
  5.4 0.7 fusion.22
  6.1 1.2 subtract_convert_fusion.1
  7.3 2.2 %pad_maximum_fusion.twf = bf16[2,4,960,256]{3,2,1,0:T(8,128)(2,1)} fusion(bf16[1,4,960,256]{3,2,1,0:T(8,128)(2,1)S(1)} %bitcast.38, bf16[1,4,960,256]{3,2,1,0:T(8,128)(2,1)S(1)} %bitcast.37), kind=kLoop, calls=%fused_computation.3 | loop fusion | flops 1966080 | bytes 7864320 | tf_op jit(solution)/shard_map/stack | solution.py:268
  9.6 0.3 fusion.39
  9.9 0.1 add.382
  9.9 0.1 add.383
  10.0 0.1 add.385
  10.1 2.2 %fusion.15 = (f32[128,960]{1,0:T(8,128)S(1)}, f32[128,960]{1,0:T(8,128)S(1)}) fusion(s32[960]{0:T(1024)S(1)} %multiply_add_fusion.1, s32[128]{0:T(128)S(1)} %add.386), kind=kLoop, calls=%fused_computation.30 | loop fusion | flops 1105920 | bytes 987392 | tf_op jit(solution)/shard_map/cos | solution.py:48
  12.3 4.4 %multiply_subtract_fusion = f32[128,16,960]{2,1,0:T(8,128)} fusion(f32[16,960]{1,0:T(8,128)S(1)} %get-tuple-element.24, f32[128,960]{1,0:T(8,128)S(1)} %get-tuple-element.20, f32[16,960]{1,0:T(8,128)S(1)} %get-tuple-element.23, f32[128,960]{1,0:T(8,128)S(1)} %get-tuple-element.19), kind=kLoop, calls=%fused_computation.2 | loop fusion | flops 5898240 | bytes 8970240 | tf_op jit(solution)/shard_map/sub | solution.py:50
  16.7 0.1 lt.76
  16.8 0.1 broadcast_in_dim.46
  16.9 0.1 add.393
  17.0 0.1 add.394
  17.1 0.1 add.399
  17.2 5.9 %fusion.twb = bf16[2048,960]{1,0:T(8,128)(2,1)} fusion(f32[128,16,960]{2,1,0:T(8,128)} %multiply_subtract_fusion, f32[2048]{0:T(1024)S(1)} %select_select_fusion), kind=kLoop, calls=%fused_computation.1 | loop fusion | flops 3932160 | bytes 11804672 | tf_op jit(solution)/shard_map/convert_element_type | solution.py:52
  23.1 0.6 cosine_multiply_fusion.2
  23.6 0.3 subtract_convert_fusion.2
  23.9 1.3 %copy.4 = bf16[576,2,288]{2,0,1:T(8,128)(2,1)} copy(bf16[576,2,288]{0,2,1:T(8,128)(2,1)S(1)} %bitcast.39) | data formatting | bytes 1327104 | tf_op jit(solution)/shard_map/reshape | solution.py:283
  25.2 0.1 add_divide_fusion
  25.3 0.1 rev.3
  25.4 0.1 broadcast_select_fusion
  25.5 0.7 fusion.56
  27.5 4.9 %divide_select_fusion = (f32[4,576,128]{2,1,0:T(8,128)}, f32[4,576,128]{2,1,0:T(8,128)}) fusion(f32[]{:T(128)} %bitcast.17, f32[]{:T(128)} %bitcast.16, f32[]{:T(128)} %bitcast.15, f32[]{:T(128)} %bitcast.14, f32[4,128]{1,0:T(4,128)S(1)} %multiply_multiply_fusion.1, f32[576]{0:T(1024)S(1)} %fusion.53, f32[]{:T(128)} %bitcast.13, f32[]{:T(128)} %bitcast.12, ...), kind=kLoop, calls=%fused_computation.21 | loop fusion | flops 6782976 | bytes 2363673 | tf_op jit(solution)/shard_map/jit(_where)/select_n | solution.py:311
  32.4 0.7 dynamic_slice.3.cpl
  33.0 84.3 %shard_map.37 = f32[3,288,960]{2,1,0:T(8,128)} custom-call(bf16[3,288,960]{2,1,0:T(8,128)(2,1)} %fusion.1.x_ref, bf16[2,4,960,256]{3,2,1,0:T(8,128)(2,1)} %pad_maximum_fusion.twf, bf16[2048,960]{1,0:T(8,128)(2,1)} %fusion.twb, bf16[2,576,288]{2,1,0:T(8,128)(2,1)} %bitcast.41, bf16[2,288,576]{2,1,0:T(8,128)(2,1)} %bitcast.40, ...), custom_call_target="tpu_custom_call" | custom-call | tf_op jit(solution)/shard_map/pallas_call | solution.py:317
  117.4 4.3 %copy.9 = f32[1,3,288,960]{3,2,1,0:T(8,128)} copy(f32[1,3,288,960]{3,2,1,0:T(8,128)} %bitcast.36) | data formatting | bytes 6635520
  (26 shorter events, 0.2 us)
Async XLA Ops:
  23.0 2.2 %copy-start.1 = (s32[4]{0:T(128)S(1)}, s32[4]{0:T(128)}, u32[]{:S(2)}) copy-start(s32[4]{0:T(128)} %param.5) | copy-start | bytes 52
  23.9 8.5 %copy-start = (bf16[24,24,576]{2,1,0:T(8,128)(2,1)}, bf16[24,24,576]{2,1,0:T(8,128)(2,1)S(1)}, u32[]{:S(2)}) copy-start(bf16[24,24,576]{2,1,0:T(8,128)(2,1)S(1)} %subtract_convert_fusion.2) | copy-start | bytes 1990660

commit v2 on v1

--- a/solution.py
+++ b/solution.py
@@ -10,6 +10,8 @@
 
 screen = 0.001
 LANES = 128
+STEP = 32
+HOP = 2
 MESH = pl.DeviceIdType.MESH
 
 
@@ -24,32 +26,19 @@
     return (products % (4 * length_all)).astype(jnp.float32) * (math.pi / (2.0 * length_all))
 
 
-def table_cells_by_modes(length_all, cell_first, cell_count, mode_ids, scales):
+def turn(length_all, products):
+    angles = angles_of(length_all, products)
+    return jnp.cos(angles), jnp.sin(angles)
+
+
+def row_table(length_all, mode_ids, scales):
     step = 24
-    mode_ids = mode_ids[..., None, :]
-    coarse = 2 * step * jnp.arange(cell_count // step, dtype=jnp.int32)[:, None]
-    fine = 2 * (cell_first + jnp.arange(step, dtype=jnp.int32))[:, None] + 1
-    angle_a = angles_of(length_all, coarse * mode_ids)
-    angle_b = angles_of(length_all, fine * mode_ids)
-    scales = scales[..., None, :]
-    cos_a, sin_a = jnp.cos(angle_a), jnp.sin(angle_a)
-    cos_b, sin_b = jnp.cos(angle_b) * scales, jnp.sin(angle_b) * scales
-    table = (
-        cos_a[..., :, None, :] * cos_b[..., None, :, :]
-        - sin_a[..., :, None, :] * sin_b[..., None, :, :]
-    )
-    return table.reshape(table.shape[:-3] + (cell_count, table.shape[-1])).astype(jnp.bfloat16)
-
-
-def table_modes_by_cells(length_all, bases, step, scales, cell_first, cell_count):
-    odd = 2 * (cell_first + jnp.arange(cell_count, dtype=jnp.int32))[None, :] + 1
-    angle_a = angles_of(length_all, bases[:, None] * odd)
-    angle_b = angles_of(length_all, jnp.arange(step, dtype=jnp.int32)[:, None] * odd)
-    cos_a, sin_a = jnp.cos(angle_a), jnp.sin(angle_a)
-    cos_b, sin_b = jnp.cos(angle_b), jnp.sin(angle_b)
-    table = cos_a[:, None] * cos_b[None] - sin_a[:, None] * sin_b[None]
-    table = table * scales[:, :, None]
-    return table.reshape(-1, cell_count).astype(jnp.bfloat16)
+    coarse = 2 * step * jnp.arange(length_all // step, dtype=jnp.int32)[:, None]
+    fine = 2 * jnp.arange(step, dtype=jnp.int32)[:, None] + 1
+    cos_a, sin_a = turn(length_all, coarse * mode_ids)
+    cos_b, sin_b = turn(length_all, fine * mode_ids)
+    table = cos_a[:, None] * (cos_b * scales) - sin_a[:, None] * (sin_b * scales)
+    return table.reshape(length_all, -1).astype(jnp.bfloat16)
 
 
 def laplace_eigen(length_all, mode_ids):
@@ -57,8 +46,8 @@
     return 4.0 * sines * sines
 
 
-def kernel(J, R, n, C, M, x_ref, twf, twb, thf, tht, dd, ee, cpl, o_ref,
-           xg, sw, sr, u, yb, yin, zin, xb, rb, rg, out,
+def kernel(J, R, n, C, M, seams, grid, fca, fsa, fcb, fsb, bca, bsa, bcb, bsb, thf, tht,
+           er, ec, own, other, o_ref, x_ref, twf, twb, dd, ee, xg, sw, sr, u, yb, yin, zin, xb, rb, rg, out,
            g_s, g_r, f_s, f_r, y_s, y_r, z_r, x_s, b_s, b_r, c_s, c_r, o_s):
     j, r, t = lax.axis_index("col"), lax.axis_index("row"), lax.axis_index("tm")
     N = C * M
@@ -69,6 +58,62 @@
     edge = p == 0
     mid = p == n // 2 - 1
 
+    half = n // 2
+    cols = seams.shape[2]
+    blocks_each = J * R * LANES // STEP
+
+    def blend(c):
+        x_ref[c] = (seams[c].astype(jnp.float32) * grid[...]).astype(jnp.bfloat16)
+
+    def build_forward(m):
+        fine = [(fcb[d, m], fsb[d, m]) for d in range(J)]
+
+        def part(a, carry):
+            at = pl.ds(pl.multiple_of(a * STEP, STEP), STEP)
+            cos_a, sin_a = fca[m, pl.ds(a, 1), :], fsa[m, pl.ds(a, 1), :]
+            for d in range(J):
+                twf[d, m, at, :] = (cos_a * fine[d][0] - sin_a * fine[d][1]).astype(jnp.bfloat16)
+            return carry
+
+        lax.fori_loop(0, cols // STEP, part, 0)
+
+    def block_of(g):
+        return bca[pl.ds(g, 1), :] * bcb[...] - bsa[pl.ds(g, 1), :] * bsb[...]
+
+    def build_backward(m):
+        def part(k, carry):
+            g = m * blocks_each + k
+            at = pl.ds(pl.multiple_of(g * STEP, STEP), STEP)
+            twb[at, :] = block_of(g).astype(jnp.bfloat16)
+            return carry
+
+        lax.fori_loop(0, blocks_each, part, 0)
+
+        @pl.when(m == 0)
+        def _():
+            first = lax.broadcasted_iota(jnp.int32, (STEP, cols), 0) == 0
+            fixed = block_of(0) * jnp.where(first, math.sqrt(0.5), 1.0)
+            twb[0:STEP, :] = fixed.astype(jnp.bfloat16)
+
+    def build_pivots(m):
+        a = er[...] + ec[m]
+
+        def sweep(chain):
+            rest, first = None, None
+            for k in range(half):
+                base = a if k == 0 else a + chain[k] * rest
+                inverse = 1.0 / (base + chain[k + 1])
+                first = inverse if k == 0 else jnp.where(p == k, inverse, first)
+                rest = base * inverse
+            return base, rest, first
+
+        base, _, first = sweep(own)
+        _, rest_other, _ = sweep(other)
+        dd[m] = first
+        ee[m] = jnp.where(p == half - 1, 1.0 / (base + own[half] * rest_other), first)
+
+    below, above = own[p], own[p + 1]
+    blend(0)
     barrier = pltpu.get_barrier_semaphore()
     for d in range(1, J):
         pl.semaphore_signal(barrier, 1, device_id={"col": lax.rem(j + d, J)}, device_id_type=MESH)
@@ -124,8 +169,12 @@
         return pltpu.make_async_copy(out.at[c], o_ref.at[c], o_s.at[c])
 
     for c in range(C):
+        if c:
+            blend(c)
         for d in range(1, J):
             gather(c, d).start()
+        if c == 0:
+            build_forward(0)
 
     def dot(a, b):
         return jnp.dot(a, b, preferred_element_type=jnp.float32)
@@ -134,6 +183,10 @@
         @pl.when(i < N)
         def _():
             c, m = i // M, i % M
+
+            @pl.when((i > 0) & (i < M))
+            def _():
+                build_forward(i)
 
             @pl.when(m == 0)
             def _():
@@ -148,6 +201,14 @@
             for d in range(1, R):
                 row_out(i, d).start()
 
+            @pl.when(i < M)
+            def _():
+                build_pivots(i)
+
+            @pl.when((i >= M) & (i < 2 * M))
+            def _():
+                build_backward(i - M)
+
         ib = i - 1
 
         @pl.when((ib >= 0) & (ib < N))
@@ -158,14 +219,14 @@
                 acc += dot(thf[lax.rem(r + R - d, R)], sr[ib, d - 1])
             u[ib] = acc
 
-        ic = i - 1 - p
+        ic = i - 1 - HOP * p
 
         @pl.when((ic >= 0) & (ic < N))
         def _():
             @pl.when(p > 0)
             def _():
                 y_inner(ic).wait_recv()
-                u[ic] = u[ic] + cpl[0] * yin[ic].astype(jnp.float32)
+                u[ic] = u[ic] + below * yin[ic].astype(jnp.float32)
             yb[ic] = (u[ic] * dd[ic % M]).astype(jnp.bfloat16)
 
             @pl.when(mid)
@@ -176,13 +237,13 @@
             def _():
                 y_inner(ic).start()
 
-        ix = i - n + p
+        ix = i - 1 - HOP * (n - 1 - p)
 
         @pl.when((ix >= 0) & (ix < N))
         def _():
             c, m = ix // M, ix % M
             x_outer(ix).wait_recv()
-            x = ((u[ix] + cpl[1] * zin[ix].astype(jnp.float32)) * ee[m]).astype(jnp.bfloat16)
+            x = ((u[ix] + above * zin[ix].astype(jnp.float32)) * ee[m]).astype(jnp.bfloat16)
             xb[ix] = x
 
             @pl.when(p > 0)
@@ -220,7 +281,7 @@
                 out_copy(c).start()
         return carry
 
-    lax.fori_loop(0, N + n + 2, step, 0)
+    lax.fori_loop(0, N + HOP * (n - 1) + 3, step, 0)
 
     def drain(i, carry):
         c, m = i // M, i % M
@@ -254,8 +315,6 @@
     grid = jnp.broadcast_to(
         grid[:, None, :, None], (levels.shape[1], tile_rows, levels.shape[2], tile_cols)
     ).reshape(rows, cols)
-    blended = (seams[0].astype(jnp.float32) * grid[None]).astype(jnp.bfloat16)
-
     modes = W // (J * R)
     M = -(-modes // LANES)
     N = C * M
@@ -265,51 +324,33 @@
     mode_f = (j * R * modes + blocks + lanes[:, None, :]).reshape(M, R * LANES)
     valid_f = jnp.broadcast_to(valid[:, None, :], (M, R, LANES)).reshape(M, R * LANES)
     scale_f = scales_of(W, mode_f, valid_f)
-    twf = jnp.stack([
-        table_cells_by_modes(W, lax.rem(j + J - d, J) * cols, cols, mode_f, scale_f)
-        for d in range(J)])
-
-    fine = 16
+    coarse = 2 * STEP * jnp.arange(cols // STEP, dtype=jnp.int32)[:, None]
+    fca, fsa = turn(W, coarse * mode_f[:, None])
+    firsts = jnp.stack([lax.rem(j + J - d, J) * cols for d in range(J)])
+    fine = 2 * (firsts[:, None] + jnp.arange(STEP, dtype=jnp.int32)) + 1
+    fcb, fsb = (v * scale_f[None, :, None] for v in turn(W, fine[:, None, :, None] * mode_f[None, :, None]))
+
     bases = (jnp.arange(J * R, dtype=jnp.int32)[:, None] * modes
-             + jnp.arange(M * LANES // fine, dtype=jnp.int32)[None, :] * fine).reshape(-1)
-    mode_b = (jnp.arange(J * R, dtype=jnp.int32)[:, None] * modes
-              + jnp.arange(M * LANES, dtype=jnp.int32)[None, :])
-    valid_b = jnp.broadcast_to(valid.reshape(1, -1), mode_b.shape)
-    scale_b = scales_of(W, mode_b, valid_b).reshape(-1, fine)
-    twb = table_modes_by_cells(W, bases, fine, scale_b, j * cols, cols)
+             + jnp.arange(M * LANES // STEP, dtype=jnp.int32)[None, :] * STEP).reshape(-1)
+    odd = 2 * (j * cols + jnp.arange(cols, dtype=jnp.int32))[None, :] + 1
+    bca, bsa = turn(W, bases[:, None] * odd)
+    bcb, bsb = (v * math.sqrt(2.0 / W) for v in turn(W, jnp.arange(STEP, dtype=jnp.int32)[:, None] * odd))
 
     mode_h = jnp.arange(H, dtype=jnp.int32)
-    tht = table_cells_by_modes(H, 0, H, mode_h, scales_of(H, mode_h))
+    tht = row_table(H, mode_h, scales_of(H, mode_h))
     thf = tht.T.reshape(H, R, rows).transpose(1, 0, 2)
     tht = tht.reshape(R, rows, H)
 
     own_modes = (j * R + r) * modes + lanes
-    a = (screen + laplace_eigen(H, mode_h)[None, :, None]
-         + laplace_eigen(W, own_modes)[:, None, :])
+    er = jnp.broadcast_to((screen + laplace_eigen(H, mode_h))[:, None], (H, LANES))
+    ec = laplace_eigen(W, own_modes)[:, None, :]
     stiff = weights.astype(jnp.float32) / 256.0
     couple = 2.0 * stiff[:-1] * stiff[1:] / (stiff[:-1] + stiff[1:])
-    half = n // 2
-    left = t < half
-    place = jnp.where(left, t, n - 1 - t)
+    left = t < n // 2
     ends = jnp.concatenate([jnp.zeros((1,), jnp.float32), couple])
     flipped = jnp.concatenate([jnp.zeros((1,), jnp.float32), couple[::-1]])
     own = jnp.where(left, ends, flipped)
     other = jnp.where(left, flipped, ends)
-
-    def sweep(chain):
-        rest = jnp.zeros_like(a)
-        first = None
-        for k in range(half):
-            base = a + chain[k] * rest
-            inverse = 1.0 / (base + chain[k + 1])
-            first = inverse if first is None else jnp.where(place == k, inverse, first)
-            rest = base * inverse
-        return base, rest, first
-
-    base, _, dd = sweep(own)
-    _, rest_other, _ = sweep(other)
-    ee = jnp.where(place == half - 1, 1.0 / (base + own[half] * rest_other), dd)
-    cpl = lax.dynamic_slice(own, (place,), (2,))
 
     bf, f32 = jnp.bfloat16, jnp.float32
     vm, dma = pltpu.VMEM, pltpu.SemaphoreType.DMA
@@ -317,9 +358,14 @@
     result = pl.pallas_call(
         functools.partial(kernel, J, R, n, C, M),
         out_shape=jax.ShapeDtypeStruct((C, rows, cols), f32),
-        in_specs=[spec] * 7 + [pl.BlockSpec(memory_space=pltpu.SMEM)],
+        in_specs=[spec] * 14 + [pl.BlockSpec(memory_space=pltpu.SMEM)] * 2,
         out_specs=pl.BlockSpec(memory_space=pl.ANY),
         scratch_shapes=[
+            vm((C, rows, cols), bf),
+            vm((J, M, cols, R * LANES), bf),
+            vm((J * R * M * LANES, cols), bf),
+            vm((M, H, LANES), f32),
+            vm((M, H, LANES), f32),
             vm((C, J - 1, rows, cols), bf),
             vm((N, R, rows, LANES), bf),
             vm((N, R - 1, rows, LANES), bf),
@@ -339,8 +385,8 @@
             dma((C,)),
         ],
         compiler_params=pltpu.CompilerParams(
-            collective_id=0, has_side_effects=True, vmem_limit_bytes=60 * 1024 * 1024),
-    )(blended, twf, twb, thf, tht, dd, ee, cpl)
+            collective_id=0, has_side_effects=True, vmem_limit_bytes=48 * 1024 * 1024),
+    )(seams[0], grid, fca, fsa, fcb, fsb, bca, bsa, bcb, bsb, thf, tht, er, ec, own, other)
     return result[None]
 
 

time: 122 us -> 94.6 us (0.78)
  other arithmetic: 27.7 us -> 9.14 us
  Pallas kernels: 84.3 us -> 71.4 us
  local copies, waits for them, and re-layouts: 8.25 us -> 13.6 us
  between operations: 1.36 us -> 0.1 us
    pallas_call x1, Pallas kernels: 84.3 us -> 71.4 us  [local(): pl.pallas_call(functools.partial(kernel, J, R, n, C, M), out_shape=jax.Sh...]
    convert_element_type x4 -> x1, other arithmetic: 10.5 us -> 0.27 us  [row_table(): return table.reshape(length_all, -1).astype(jnp.bfloat16)]
    unnamed x6 -> x14, local copies, waits for them, and re-layouts: 4.29 us -> 9.83 us
    select_n x1 -> x0, other arithmetic: 4.92 us -> none  [local(): ee = jnp.where(place == half - 1, 1.0 / (base + own[half] * rest_other), dd)]
    sub x1 -> x0, other arithmetic: 4.39 us -> none  [table_modes_by_cells(): table = cos_a[:, None] * cos_b[None] - sin_a[:, None] * sin_b[None]]
    cos x3 -> x0, other arithmetic: 3.2 us -> none  [the longest x1 2.18 us: table_modes_by_cells(): cos_a, sin_a = (jnp.cos(angle_a), jnp.sin(angle_a))]
    sin x0 -> x2, other arithmetic: none -> 3.16 us  [turn(): return (jnp.cos(angles), jnp.sin(angles))]
    mul x5 -> x6, other arithmetic: 1.47 us -> 3.82 us  [the longest x1 1.98 us: local(): v * scale_f[None, :, None]]
where the time goes in v2:
time: 94.6 us; the launch traced here: 94.2 us
  Pallas kernels  71.4 us (75%)
  local copies, waits for them, and re-layouts  13.6 us (14%)
  other arithmetic  9.14 us (10%)
    pallas_call x1, Pallas kernels, local(): pl.pallas_call(functools.partial(kernel, J, R, n, C, M), out_shape=jax.Sh...  71.4 us
    unnamed x14, local copies, waits for them, and re-layouts  9.83 us
    sin x2, other arithmetic, turn(): return (jnp.cos(angles), jnp.sin(angles))  3.16 us
    mul x1, other arithmetic, local(): v * scale_f[None, :, None]  1.98 us

profile of v2, /device:TPU:1, one launch (start us, length us, event | category | flops | bytes accessed | tf_op | source)
XLA Modules:
  0.0 94.2 jit_solution(1684455653727470259)
XLA Ops:
  0.0 0.1 pad_add_fusion
  0.1 0.7 convert_multiply_fusion
  0.7 0.1 add_divide_fusion
  0.8 0.1 rev.3
  0.9 0.1 broadcast_select_fusion
  1.0 0.1 multiply_add_fusion.2
  1.1 0.1 broadcast_bitcast_fusion.1
  1.2 0.1 broadcast_add_fusion
  1.3 0.1 add.246
  1.3 0.1 multiply_multiply_fusion.1.ec
  1.4 0.7 multiply_bitcast_fusion
  2.2 0.6 cosine_multiply_fusion.2
  2.8 1.3 %fusion.20 = (f32[4,30,256]{2,1,0:T(8,128)S(1)}, f32[4,30,256]{2,1,0:T(8,128)}) fusion(s32[4,256]{1,0:T(4,128)S(1)} %get-tuple-element.6, s32[30]{0:T(128)S(1)} %iota_multiply_fusion.3), kind=kLoop, calls=%fused_computation.33 | loop fusion | flops 276480 | bytes 249976 | tf_op jit(solution)/shard_map/sin | solution.py:31
  4.1 1.2 %sine_multiply_fusion.1 = (f32[32,960]{1,0:T(8,128)}, f32[32,960]{1,0:T(8,128)}) fusion(s32[960]{0:T(1024)S(1)} %multiply_add_fusion), kind=kLoop, calls=%fused_computation.25 | loop fusion | flops 337920 | bytes 249600 | tf_op jit(solution)/shard_map/mul | solution.py:337
  5.3 0.1 broadcast_in_dim.35.er
  5.5 0.3 subtract_convert_fusion
  5.7 2.0 %sine_multiply_fusion = (f32[2,4,32,256]{3,2,1,0:T(8,128)}, f32[2,4,32,256]{3,2,1,0:T(8,128)}) fusion(f32[4,256]{1,0:T(4,128)S(1)} %get-tuple-element.5, s32[4,256]{1,0:T(4,128)S(1)} %get-tuple-element.6, s32[2,32]{1,0:T(2,128)S(1)} %multiply_add_fusion.2), kind=kLoop, calls=%fused_computation.12 | loop fusion | flops 720896 | bytes 532736 | tf_op jit(solution)/shard_map/mul | solution.py:331
  7.7 1.9 %fusion.6 = (f32[64,960]{1,0:T(8,128)S(1)}, f32[64,960]{1,0:T(8,128)}) fusion(s32[960]{0:T(1024)S(1)} %multiply_add_fusion, s32[64]{0:T(128)S(1)} %add.246), kind=kLoop, calls=%fused_computation.10 | loop fusion | flops 552960 | bytes 495616 | tf_op jit(solution)/shard_map/sin | solution.py:31
  9.6 0.6 copy.5
  10.2 1.2 %broadcast_in_dim.26 = f32[4,72,8,120]{3,2,1,0:T(8,128)} broadcast(f32[4,8]{1,0:T(4,128)S(1)} %multiply_bitcast_fusion), dimensions={0,2} | broadcast | bytes 1106048 | tf_op jit(solution)/shard_map/broadcast_in_dim | solution.py:315
  11.3 1.7 %reshape.353.grid = f32[288,960]{1,0:T(8,128)S(1)} reshape(f32[4,72,8,120]{3,2,1,0:T(8,128)} %broadcast_in_dim.26) | data formatting | bytes 2211840 | tf_op jit(solution)/shard_map/reshape | solution.py:317
  13.0 0.0 copy-start
  13.0 0.9 copy-done
  14.0 0.0 copy-start.1
  14.0 0.9 %copy-done.1 = f32[2,4,32,256]{3,2,1,0:T(8,128)S(1)} copy-done((f32[2,4,32,256]{3,2,1,0:T(8,128)S(1)}, f32[2,4,32,256]{3,2,1,0:T(8,128)}, u32[]{:S(2)}) %copy-start.1) | copy-done | bytes 262168
  14.9 0.0 copy-start.2
  14.9 0.9 %copy-done.2 = f32[2,4,32,256]{3,2,1,0:T(8,128)S(1)} copy-done((f32[2,4,32,256]{3,2,1,0:T(8,128)S(1)}, f32[2,4,32,256]{3,2,1,0:T(8,128)}, u32[]{:S(2)}) %copy-start.2) | copy-done | bytes 262168
  15.9 0.9 copy-done.3
  16.8 0.9 copy-done.4
  17.7 0.9 copy-done.5
  18.6 71.4 %shard_map.37 = f32[3,288,960]{2,1,0:T(8,128)} custom-call(bf16[3,288,960]{2,1,0:T(8,128)(2,1)} %bitcast.29, f32[288,960]{1,0:T(8,128)S(1)} %reshape.353.grid, f32[4,30,256]{2,1,0:T(8,128)S(1)} %copy-done.3, f32[4,30,256]{2,1,0:T(8,128)S(1)} %get-tuple-element.13.fsa, f32[2,4,32,256]{3,2,1,0:T(8,128)S(1)} %copy-done.2, f32[2,4,32,256]{3,2,1,0:T(8,128)S(1)} %copy-done.1, ...), custom_call_target="tpu_custom_call" | custom-call | tf_op jit(solution)/shard_map/pallas_call | solution.py:358
  90.0 4.3 %copy.11 = f32[1,3,288,960]{3,2,1,0:T(8,128)} copy(f32[1,3,288,960]{3,2,1,0:T(8,128)} %bitcast.28) | data formatting | bytes 6635520
  (17 shorter events, 0.1 us)
Async XLA Ops:
  13.0 1.0 %copy-start = (f32[64,960]{1,0:T(8,128)S(1)}, f32[64,960]{1,0:T(8,128)}, u32[]{:S(2)}) copy-start(f32[64,960]{1,0:T(8,128)} %get-tuple-element.12.bca) | copy-start | bytes 737284
  14.0 0.9 %copy-start.1 = (f32[2,4,32,256]{3,2,1,0:T(8,128)S(1)}, f32[2,4,32,256]{3,2,1,0:T(8,128)}, u32[]{:S(2)}) copy-start(f32[2,4,32,256]{3,2,1,0:T(8,128)} %get-tuple-element.7.fsb) | copy-start | bytes 786436
  14.9 0.9 %copy-start.2 = (f32[2,4,32,256]{3,2,1,0:T(8,128)S(1)}, f32[2,4,32,256]{3,2,1,0:T(8,128)}, u32[]{:S(2)}) copy-start(f32[2,4,32,256]{3,2,1,0:T(8,128)} %get-tuple-element.8.fcb) | copy-start | bytes 786436
  15.9 0.9 copy-start.3
  16.8 0.9 copy-start.4
  17.7 0.9 copy-start.5
